TPU v7x, 256 devices: a whole 4x4x8 slice. The times are simulated.
256 devices in a mesh: dp: 2 (over core), tensor: 8 (over z), expert: 16 (over y, x).
Axes of the slice: x: 4, y: 4, z: 8, core: 2. Of those that a mesh axis runs over, the one named last changes fastest.
Arguments:
- attn_heads: bfloat16 [32, 64, 4096], P(('dp', 'expert'), None, 'tensor'), may hold values from -6 to 6
- out_proj: bfloat16 [4096, 4096], P('tensor'), may hold values from -0.09375 to 0.09375
- residual: bfloat16 [32, 64, 4096], P(('dp', 'expert'), 'tensor'), may hold values from -6 to 6
- norm_gain: float32 [4096], replicated, may hold values from 0.25 to 1.75
- expert_ids: int32 [32, 64, 8], P(('dp', 'expert'), 'tensor'), may hold values from 0 to 15, all different within a row; in each aligned block of 8 rows (0 to 7, 8 to 15, ..., all dimensions but the last counted through in order) at most 6 rows name the same one
- weight_codes: int32 [32, 64, 8], P(('dp', 'expert'), 'tensor'), may hold values from 1 to 16
- w_gate: bfloat16 [16, 1536, 4096], P('expert', 'tensor'), may hold values from -0.09375 to 0.09375
- w_up: bfloat16 [16, 1536, 4096], P('expert', 'tensor'), may hold values from -0.09375 to 0.09375
- w_down: bfloat16 [16, 1536, 4096], P('expert', 'tensor'), may hold values from -0.625 to 0.625
Outputs:
- layer_out: bfloat16 [32, 64, 4096], P(('dp', 'expert'), 'tensor')
Inputs may be any that keep to these rules, and one draw needn't show every extreme that they name: `expert_ids`: each token names 8 different experts. Among the 8 consecutive tokens of one device (aligned blocks of the flattened first two dimensions) no expert is named by more than 6 rows, and every draw has an expert named exactly 6 times in some device's rows.
All inputs are finite; a program needn't handle non-finite values.
Results may differ from a plain program's by a relative error of at most 0.022.
Values may be sent and summed in bfloat16 or wider, within the bound.
No kernel may reach another device: no remote copies, remote signals or barrier semaphores. Data moves between devices by JAX's collectives and lax.ppermute only.
A program may use at most 128 MiB of HBM per device.

v0:
```python
import jax
import jax.numpy as jnp
from jax import lax
from jax.sharding import PartitionSpec as P

EXPERTS = 16
TOP = 8
CAP = 6


def normalize(hidden, norm_gain):
    mean_square = jnp.mean(hidden * hidden, axis=-1, keepdims=True)
    return (hidden * lax.rsqrt(mean_square + 1e-06) * norm_gain).astype(jnp.bfloat16)


def place_rows(route_ids, per_device):
    flat_rows = route_ids.reshape(-1)
    one_hot = (flat_rows[:, None] == jnp.arange(EXPERTS, dtype=jnp.int32)[None, :]).astype(
        jnp.int32
    )
    position = jnp.sum((jnp.cumsum(one_hot, axis=0) - one_hot) * one_hot, axis=1)
    owner_dev = flat_rows // per_device
    local_expert = flat_rows % per_device
    slot_index = owner_dev * (CAP * per_device) + position * per_device + local_expert
    return slot_index.reshape(route_ids.shape)


def build_outgoing(normed, slot_index, slot_count):
    placement = jnp.any(
        slot_index[None, :, :] == jnp.arange(slot_count, dtype=jnp.int32)[:, None, None], axis=2
    )
    return jnp.dot(
        placement.astype(jnp.bfloat16), normed, preferred_element_type=jnp.float32
    ).astype(jnp.bfloat16)


def on_device(
    attn_heads, out_proj, residual, norm_gain, expert_ids, weight_codes, w_gate, w_up, w_down
):
    tensor_count = lax.axis_size("tensor")
    expert_count = lax.axis_size("expert")
    per_device = w_gate.shape[0]
    head_rows = attn_heads[0]
    own_residual = residual[0]
    own_ids = expert_ids[0]
    own_codes = weight_codes[0]
    tok_own = own_residual.shape[0]
    model_width = own_residual.shape[1]
    slot_count = expert_count * CAP * per_device
    attn_sum = lax.psum_scatter(
        jnp.dot(head_rows, out_proj, preferred_element_type=jnp.float32).astype(jnp.bfloat16),
        "tensor",
        scatter_dimension=0,
        tiled=True,
    ).astype(jnp.float32)
    hidden = own_residual.astype(jnp.float32) + attn_sum
    normed = normalize(hidden, norm_gain)
    slot_index = place_rows(own_ids, per_device)
    outgoing = build_outgoing(normed, slot_index, slot_count).reshape(
        expert_count, CAP * per_device, model_width
    )
    arrived = lax.all_to_all(outgoing, "expert", split_axis=0, concat_axis=0, tiled=True)
    arrived = arrived.reshape(expert_count * CAP, per_device, model_width)
    portion = lax.all_gather(arrived, "tensor", axis=0, tiled=True)
    gate_value = jnp.einsum("red,efd->ref", portion, w_gate, preferred_element_type=jnp.float32)
    up_value = jnp.einsum("red,efd->ref", portion, w_up, preferred_element_type=jnp.float32)
    activated = (jax.nn.silu(gate_value) * up_value).astype(jnp.bfloat16)
    partial_out = jnp.einsum("ref,efd->red", activated, w_down, preferred_element_type=jnp.float32)
    partial_out = partial_out.astype(jnp.bfloat16).reshape(
        tensor_count * expert_count, CAP * per_device, model_width
    )
    received = lax.all_to_all(
        partial_out, ("tensor", "expert"), split_axis=0, concat_axis=0, tiled=True
    )
    received = received.reshape(tensor_count, slot_count, model_width)
    returned_flat = jnp.sum(received, axis=0, dtype=jnp.float32).astype(jnp.bfloat16)
    picked = jnp.take(returned_flat, slot_index.reshape(-1), axis=0).reshape(
        tok_own, TOP, model_width
    )
    code_values = own_codes.astype(jnp.float32)
    mixing = code_values / jnp.sum(code_values, axis=-1, keepdims=True)
    expert_mix = jnp.sum(mixing[:, :, None] * picked.astype(jnp.float32), axis=1)
    layer_out = (hidden + expert_mix).astype(jnp.bfloat16)
    return layer_out[None]


def solution(mesh):
    return jax.shard_map(
        on_device,
        mesh=mesh,
        in_specs=(
            P(("dp", "expert"), None, "tensor"),
            P("tensor", None),
            P(("dp", "expert"), "tensor", None),
            P(),
            P(("dp", "expert"), "tensor", None),
            P(("dp", "expert"), "tensor", None),
            P("expert", "tensor", None),
            P("expert", "tensor", None),
            P("expert", "tensor", None),
        ),
        out_specs=P(("dp", "expert"), "tensor", None),
        check_vma=False,
    )
```

profile of v0, /device:TPU:6, one launch (start us, length us, event | category | flops | bytes accessed | tf_op | source)
XLA Modules:
  0.0 396.0 jit_solution(4905630625477676545)
XLA Ops:
  6.5 0.0 copy-start
  6.5 0.0 copy-start.4
  6.5 0.0 copy-start.2
  6.5 0.0 copy-start.5
  6.5 0.0 reduce-scatter.2.cloned.1.call-start
  6.6 4.0 %convolution_convert_fusion.2 = bf16[64,4096]{1,0:T(8,128)(2,1)} fusion(bf16[512,4096]{1,0:T(8,128)(2,1)} %param.10, bf16[1,64,512]{2,1,0:T(8,128)(2,1)} %param.9), kind=kOutput, calls=%fused_computation.8 | convolution fusion | flops 268697600 | bytes 4784128 | tf_op jit(solution)/shard_map/dot_general | solution.py:51
  10.6 0.0 reduce-scatter.2.cloned.1.call-update
  10.6 0.0 all-gather.2.cloned.1.call-start
  10.6 0.0 copy-done.4
  10.6 0.1 reshape_squeeze.3
  10.7 0.1 fusion.48
  10.8 0.1 reduce_window_sum.11
  10.9 0.2 select_reduce_fusion
  11.1 0.1 reduce_sum.57
  11.2 0.1 fusion.49
  11.3 39.6 %reduce-scatter.2.cloned.1.call-done = bf16[8,4096]{1,0:T(8,128)(2,1)} async-done(((bf16[64,4096]{1,0:T(8,128)(2,1)}), bf16[8,4096]{1,0:T(8,128)(2,1)}) %reduce-scatter.2.cloned.1.call-update) | async-done | bytes 65552 | tf_op jit(solution)/shard_map/reduce_scatter | solution.py:50
  50.9 0.0 copy-done.2
  50.9 1.0 multiply_reduce_fusion.1
  51.9 0.0 copy-done.5
  51.9 1.3 convolution_convert_fusion.1
  53.1 0.3 reshape.115
  53.4 17.6 %all_to_all.10 = bf16[16,6,4096]{2,1,0:T(8,128)(2,1)} all-to-all(bf16[16,6,4096]{2,1,0:T(8,128)(2,1)S(1)} %reshape.115), channel_id=1, replica_groups=mesh['dp'=2,'tensor'=8,'expert'=16] {'expert'}, dimensions={0} | all-to-all | bytes 1572864 | tf_op jit(solution)/shard_map/all_to_all | solution.py:62
  71.0 2.2 reshape.116
  73.2 0.0 all-gather.2.cloned.1.call-update
  73.2 0.0 copy-start.1
  73.2 71.8 %all-gather.2.cloned.1.call-done = bf16[768,1,4096]{2,0,1:T(8,128)(2,1)} async-done(((bf16[96,1,4096]{2,0,1:T(8,128)(2,1)}), bf16[768,1,4096]{2,0,1:T(8,128)(2,1)}) %all-gather.2.cloned.1.call-update) | async-done | bytes 6291472 | tf_op jit(solution)/shard_map/all_gather | solution.py:64
  145.0 6.3 %fusion.8 = f32[768,1,192]{0,2,1:T(8,128)} fusion(bf16[1,192,4096]{2,1,0:T(8,128)(2,1)} %param.15, bf16[768,1,4096]{2,0,1:T(8,128)(2,1)} %all-gather.2.cloned.1.call-done), kind=kOutput, calls=%fused_computation.12 | convolution fusion | flops 1207959552 | bytes 8454144 | tf_op jit(solution)/shard_map/red,efd->ref/dot_general | solution.py:65
  151.3 0.0 copy-done
  151.3 0.0 copy-done.1
  151.3 13.0 %fusion.4 = bf16[768,1,4096]{2,0,1:T(8,128)(2,1)} fusion(bf16[1,192,4096]{2,1,0:T(8,128)(2,1)S(1)} %copy-done, bf16[1,192,4096]{2,1,0:T(8,128)(2,1)S(1)} %copy-done.1, bf16[768,1,4096]{2,0,1:T(8,128)(2,1)} %all-gather.2.cloned.1.call-done, f32[768,1,192]{0,2,1:T(8,128)} %fusion.8), kind=kOutput, calls=%fused_computation.6 | convolution fusion | flops 2419949568 | bytes 16318464 | tf_op jit(solution)/shard_map/ref,efd->red/dot_general | solution.py:68
  164.3 10.1 %reshape.122 = bf16[128,6,4096]{2,1,0:T(8,128)(2,1)} reshape(bf16[768,1,4096]{2,0,1:T(8,128)(2,1)} %fusion.4) | data formatting | bytes 12582912 | tf_op jit(solution)/shard_map/reshape | solution.py:69
  174.4 0.0 copy-start.6
  174.4 11.7 %all-to-all-start.1 = ((bf16[128,6,4096]{2,1,0:T(8,128)(2,1)}), bf16[128,6,4096]{2,1,0:T(8,128)(2,1)}, u32[]{:S(2)}, u32[]{:S(2)}) async-start(bf16[128,6,4096]{2,1,0:T(8,128)(2,1)} %reshape.122), calls=%async_computation.2 | async-start | bytes 16777216 | tf_op jit(solution)/shard_map/all_to_all | solution.py:72
  186.1 0.1 reduce_sum.56
  186.2 0.1 mul.72
  186.3 0.0 copy-done.6
  186.3 0.1 convert_reduce_fusion
  186.4 0.1 bitcast_divide_fusion
  186.5 186.5 %all-to-all-done.1 = bf16[128,6,4096]{2,1,0:T(8,128)(2,1)} async-done(((bf16[128,6,4096]{2,1,0:T(8,128)(2,1)}), bf16[128,6,4096]{2,1,0:T(8,128)(2,1)}, u32[]{:S(2)}, u32[]{:S(2)}) %all-to-all-start.1) | async-done | bytes 6291488 | tf_op jit(solution)/shard_map/all_to_all | solution.py:72
  373.0 10.2 %reshape.123 = bf16[8,96,4096]{2,1,0:T(8,128)(2,1)} reshape(bf16[128,6,4096]{2,1,0:T(8,128)(2,1)} %all-to-all-done.1) | data formatting | bytes 12582912 | tf_op jit(solution)/shard_map/reshape | solution.py:75
  383.2 4.0 %reduce_sum.59 = bf16[96,4096]{1,0:T(8,128)(2,1)S(1)} reduce(bf16[8,96,4096]{2,1,0:T(8,128)(2,1)} %reshape.123, bf16[]{:T(256)} %constant.65.clone.1), dimensions={0}, to_apply=%region_6.7 | reduce | flops 2752512 | bytes 7077890 | tf_op jit(solution)/shard_map/reduce_sum | solution.py:76
  387.1 0.0 copy-start.3
  387.2 0.9 gather_fusion
  388.0 0.4 multiply_reduce_fusion
  388.5 0.0 copy-done.3
  388.5 0.7 fusion.43
  (5 shorter events, 0.0 us)
Async XLA Ops:
  6.5 144.8 %copy-start = (bf16[1,192,4096]{2,1,0:T(8,128)(2,1)S(1)}, bf16[1,192,4096]{2,1,0:T(8,128)(2,1)}, u32[]{:S(2)}) copy-start(bf16[1,192,4096]{2,1,0:T(8,128)(2,1)} %param.17) | copy-start | bytes 4718596
  6.5 4.1 %copy-start.4 = (s32[1,8,8]{2,1,0:T(8,128)S(1)}, s32[1,8,8]{2,1,0:T(8,128)}, u32[]{:S(2)}) copy-start(s32[1,8,8]{2,1,0:T(8,128)} %param.13) | copy-start | bytes 772
  6.5 44.3 %copy-start.2 = (bf16[1,8,4096]{2,1,0:T(8,128)(2,1)S(1)}, bf16[1,8,4096]{2,1,0:T(8,128)(2,1)}, u32[]{:S(2)}) copy-start(bf16[1,8,4096]{2,1,0:T(8,128)(2,1)} %param.11) | copy-start | bytes 196612
  6.5 45.3 %copy-start.5 = (f32[4096]{0:T(1024)S(1)}, f32[4096]{0:T(1024)}, u32[]{:S(2)}) copy-start(f32[4096]{0:T(1024)} %param.12) | copy-start | bytes 49156
  6.5 44.3 %reduce-scatter.2.cloned.1.call-start = ((), (), s32[]{:S(2)}) async-start(), calls=%async_computation.3 | async-start | bytes 589824 | tf_op jit(solution)/shard_map/reduce_scatter | solution.py:50
  10.6 134.4 %all-gather.2.cloned.1.call-start = ((), (), s32[]{:S(2)}) async-start(), calls=%async_computation.4 | async-start | bytes 7077888 | tf_op jit(solution)/shard_map/all_gather | solution.py:64
  73.2 78.1 %copy-start.1 = (bf16[1,192,4096]{2,1,0:T(8,128)(2,1)S(1)}, bf16[1,192,4096]{2,1,0:T(8,128)(2,1)}, u32[]{:S(2)}) copy-start(bf16[1,192,4096]{2,1,0:T(8,128)(2,1)} %param.16) | copy-start | bytes 4718596
  174.4 11.9 %copy-start.6 = (s32[1,8,8]{2,1,0:T(8,128)S(1)}, s32[1,8,8]{2,1,0:T(8,128)}, u32[]{:S(2)}) copy-start(s32[1,8,8]{2,1,0:T(8,128)} %param.14) | copy-start | bytes 772
  174.4 198.5 %all-to-all-start.1 = ((bf16[128,6,4096]{2,1,0:T(8,128)(2,1)}), bf16[128,6,4096]{2,1,0:T(8,128)(2,1)}, u32[]{:S(2)}, u32[]{:S(2)}) async-start(bf16[128,6,4096]{2,1,0:T(8,128)(2,1)} %reshape.122), calls=%async_computation.2 | async-start | bytes 16777216 | tf_op jit(solution)/shard_map/all_to_all | solution.py:72
  387.1 1.3 copy-start.3
Sparse Core Ops, SparseCore 0:
  10.7 40.1 reduce-scatter.1
  73.3 71.6 all-gather.1
where the time goes:
time: 397 us; the launch traced here: 396 us
  waiting for transfers between devices  298 us (75%)
  matrix products  24.6 us (6%)
  local copies, waits for them, and re-layouts  24 us (6%)
  blocking collectives  17.6 us (4%)
  between operations  13.5 us (3%)
  starting transfers between devices  11.8 us (3%)
  other arithmetic  6.73 us (2%)
    all_to_all x1, waiting for transfers between devices, on_device(): lax.all_to_all(partial_out, ('tensor', 'expert'), split_axis=0, concat_ax...  186 us
    all_gather x1, waiting for transfers between devices, on_device(): portion = lax.all_gather(arrived, 'tensor', axis=0, tiled=True)  71.8 us
    reduce_scatter x1, waiting for transfers between devices, on_device(): lax.psum_scatter(jnp.dot(head_rows, out_proj, preferred_element_type=jnp....  39.6 us
    all_to_all x1, blocking collectives, on_device(): lax.all_to_all(outgoing, 'expert', split_axis=0, concat_axis=0, tiled=True)  17.6 us
    dot_general x1, matrix products, on_device(): jnp.einsum('ref,efd->red', activated, w_down, preferred_element_type=jnp....  13 us
    all_to_all x1, starting transfers between devices, on_device(): lax.all_to_all(partial_out, ('tensor', 'expert'), split_axis=0, concat_ax...  11.7 us
    reshape x1, local copies, waits for them, and re-layouts, on_device(): received = received.reshape(tensor_count, slot_count, model_width)  10.2 us
    reshape x1, local copies, waits for them, and re-layouts, on_device(): partial_out.astype(jnp.bfloat16)  10.1 us
  transfers between devices with their start and end apart: 3, of which 3 were waited for; matrix products, arithmetic and copies ran while one was open for 0% of the time, Pallas kernels for 0%

commit v1 on v0

--- a/solution.py
+++ b/solution.py
@@ -61,7 +61,16 @@
     )
     arrived = lax.all_to_all(outgoing, "expert", split_axis=0, concat_axis=0, tiled=True)
     arrived = arrived.reshape(expert_count * CAP, per_device, model_width)
-    portion = lax.all_gather(arrived, "tensor", axis=0, tiled=True)
+    ways = lax.axis_size("tensor")
+    up = [(d, (d + 1) % ways) for d in range(ways)]
+    down = [(d, (d - 1) % ways) for d in range(ways)]
+    earlier, later = ([arrived], [arrived])
+    for _ in range(ways // 2):
+        earlier.append(lax.ppermute(earlier[-1], "tensor", up))
+    for _ in range((ways - 1) // 2):
+        later.append(lax.ppermute(later[-1], "tensor", down))
+    line = jnp.concatenate([*earlier[::-1], *later[1:]], axis=0)
+    portion = jnp.roll(line, (lax.axis_index("tensor") - ways // 2) * arrived.shape[0], axis=0)
     gate_value = jnp.einsum("red,efd->ref", portion, w_gate, preferred_element_type=jnp.float32)
     up_value = jnp.einsum("red,efd->ref", portion, w_up, preferred_element_type=jnp.float32)
     activated = (jax.nn.silu(gate_value) * up_value).astype(jnp.bfloat16)

time: 397 us -> 392 us (0.987)
  waiting for transfers between devices: 298 us -> 269 us
  local copies, waits for them, and re-layouts: 24 us -> 40.4 us
  starting transfers between devices: 11.8 us -> 19.9 us
    all_gather x1 -> x0, waiting for transfers between devices: 71.8 us -> none  [on_device(): portion = lax.all_gather(arrived, 'tensor', axis=0, tiled=True)]
    ppermute x0 -> x7, waiting for transfers between devices: none -> 56.7 us  [the longest x4 56 us: on_device(): earlier.append(lax.ppermute(earlier[-1], 'tensor', up))]
    unnamed x14 -> x33, local copies, waits for them, and re-layouts: 0.03 us -> 16.5 us
    all_to_all x1, waiting for transfers between devices: 186 us -> 174 us  [on_device(): lax.all_to_all(partial_out, ('tensor', 'expert'), split_axis=0, concat_ax...]
    ppermute x0 -> x7, starting transfers between devices: none -> 9.76 us  [the longest x3 8.8 us: on_device(): later.append(lax.ppermute(later[-1], 'tensor', down))]
    dot_general x1, matrix products: 6.29 us -> 2.21 us  [on_device(): jnp.einsum('red,efd->ref', portion, w_gate, preferred_element_type=jnp.fl...]
  transfers between devices with their start and end apart: 3 -> 9, of which waited for: 3 -> 7; matrix products, arithmetic and copies ran while one was open for 0% -> 2% of each run, Pallas kernels for 0% -> 0%
where the time goes in v1:
time: 392 us; the launch traced here: 389 us
  waiting for transfers between devices  269 us (69%)
  local copies, waits for them, and re-layouts  40.4 us (10%)
  matrix products  20.8 us (5%)
  starting transfers between devices  19.9 us (5%)
  blocking collectives  17.6 us (4%)
  between operations  13.7 us (3%)
  other arithmetic  7.44 us (2%)
    all_to_all x1, waiting for transfers between devices, on_device(): lax.all_to_all(partial_out, ('tensor', 'expert'), split_axis=0, concat_ax...  174 us
    ppermute x4, waiting for transfers between devices, on_device(): earlier.append(lax.ppermute(earlier[-1], 'tensor', up))  56 us
    reduce_scatter x1, waiting for transfers between devices, on_device(): lax.psum_scatter(jnp.dot(head_rows, out_proj, preferred_element_type=jnp....  38.3 us
    all_to_all x1, blocking collectives, on_device(): lax.all_to_all(outgoing, 'expert', split_axis=0, concat_axis=0, tiled=True)  17.6 us
    unnamed x33, local copies, waits for them, and re-layouts  16.5 us
    dot_general x1, matrix products, on_device(): jnp.einsum('ref,efd->red', activated, w_down, preferred_element_type=jnp....  13.4 us
    reshape x1, local copies, waits for them, and re-layouts, on_device(): received = received.reshape(tensor_count, slot_count, model_width)  10.2 us
    reshape x1, local copies, waits for them, and re-layouts, on_device(): partial_out.astype(jnp.bfloat16)  10.2 us
  transfers between devices with their start and end apart: 9, of which 7 were waited for; matrix products, arithmetic and copies ran while one was open for 2% of the time, Pallas kernels for 0%

profile of v1, /device:TPU:6, one launch (start us, length us, event | category | flops | bytes accessed | tf_op | source)
XLA Modules:
  0.0 389.2 jit_solution(11748759291753001979)
XLA Ops:
  6.5 4.0 %convolution_convert_fusion.2 = bf16[64,4096]{1,0:T(8,128)(2,1)} fusion(bf16[512,4096]{1,0:T(8,128)(2,1)} %param.10, bf16[1,64,512]{2,1,0:T(8,128)(2,1)} %param.9), kind=kOutput, calls=%fused_computation.10 | convolution fusion | flops 268697600 | bytes 4784128 | tf_op jit(solution)/shard_map/dot_general | solution.py:51
  10.5 0.0 reduce-scatter.2.cloned.1.call-update
  10.5 0.8 reshape_squeeze.3
  11.3 0.1 fusion.26
  11.4 0.1 reduce_window_sum.11
  11.5 0.2 select_reduce_fusion
  11.7 0.1 reduce_sum.57
  11.7 0.7 broadcast_multiply_fusion
  12.4 0.1 fusion.27
  12.5 38.3 %reduce-scatter.2.cloned.1.call-done = bf16[8,4096]{1,0:T(8,128)(2,1)} async-done(((bf16[64,4096]{1,0:T(8,128)(2,1)}), bf16[8,4096]{1,0:T(8,128)(2,1)}) %reduce-scatter.2.cloned.1.call-update) | async-done | bytes 65552 | tf_op jit(solution)/shard_map/reduce_scatter | solution.py:50
  50.8 1.0 multiply_reduce_fusion.1
  51.8 1.3 convolution_convert_fusion.1
  53.1 0.3 reshape.115
  53.4 17.6 %all_to_all.10 = bf16[16,6,4096]{2,1,0:T(8,128)(2,1)} all-to-all(bf16[16,6,4096]{2,1,0:T(8,128)(2,1)S(1)} %reshape.115), channel_id=1, replica_groups=mesh['dp'=2,'tensor'=8,'expert'=16] {'expert'}, dimensions={0} | all-to-all | bytes 1572864 | tf_op jit(solution)/shard_map/all_to_all | solution.py:62
  71.0 1.4 reshape.116
  72.5 0.9 collective-permute-start
  73.4 16.8 %collective-permute-done = bf16[96,1,4096]{2,0,1:T(8,128)(2,1)S(1)} collective-permute-done((bf16[96,1,4096]{2,0,1:T(8,128)(2,1)S(1)}, bf16[96,1,4096]{2,0,1:T(8,128)(2,1)S(1)}, u32[]{:S(2)}, u32[]{:S(2)}) %collective-permute-start) | collective-permute-done | bytes 786464 | tf_op jit(solution)/shard_map/ppermute | solution.py:69
  90.2 0.0 collective-permute-start.1
  90.2 3.2 collective-permute-start.4
  93.5 14.5 %collective-permute-done.1 = bf16[96,1,4096]{2,0,1:T(8,128)(2,1)S(1)} collective-permute-done((bf16[96,1,4096]{2,0,1:T(8,128)(2,1)S(1)}, bf16[96,1,4096]{2,0,1:T(8,128)(2,1)S(1)}, u32[]{:S(2)}, u32[]{:S(2)}) %collective-permute-start.1) | collective-permute-done | bytes 786464 | tf_op jit(solution)/shard_map/ppermute | solution.py:69
  108.0 0.0 collective-permute-start.2
  108.0 0.0 collective-permute-done.4
  108.0 0.9 copy-done.2
  108.8 2.4 collective-permute-start.5
  111.2 15.1 %collective-permute-done.2 = bf16[96,1,4096]{2,0,1:T(8,128)(2,1)} collective-permute-done((bf16[96,1,4096]{2,0,1:T(8,128)(2,1)S(1)}, bf16[96,1,4096]{2,0,1:T(8,128)(2,1)}, u32[]{:S(2)}, u32[]{:S(2)}) %collective-permute-start.2) | collective-permute-done | bytes 786464 | tf_op jit(solution)/shard_map/ppermute | solution.py:69
  126.3 0.0 collective-permute-start.3
  126.3 0.7 collective-permute-done.5
  127.0 3.2 collective-permute-start.6
  130.2 9.6 %collective-permute-done.3 = bf16[96,1,4096]{2,0,1:T(8,128)(2,1)} collective-permute-done((bf16[96,1,4096]{2,0,1:T(8,128)(2,1)}, bf16[96,1,4096]{2,0,1:T(8,128)(2,1)}, u32[]{:S(2)}, u32[]{:S(2)}) %collective-permute-start.3) | collective-permute-done | bytes 786464 | tf_op jit(solution)/shard_map/ppermute | solution.py:69
  139.8 1.2 constant_dynamic-update-slice_fusion.15
  141.0 1.2 constant_dynamic-update-slice_fusion.14
  142.2 1.2 constant_dynamic-update-slice_fusion.13
  143.4 0.1 constant_dynamic-update-slice_fusion.12
  143.4 0.1 constant_dynamic-update-slice_fusion.11
  143.5 1.2 constant_dynamic-update-slice_fusion.10
  144.7 1.2 constant_dynamic-update-slice_fusion.9
  145.9 0.0 collective-permute-done.6
  145.9 0.1 constant_dynamic-update-slice_fusion.8
  146.0 1.2 constant_dynamic-update-slice_fusion.7
  147.1 1.2 constant_dynamic-update-slice_fusion.6
  148.3 0.1 constant_dynamic-update-slice_fusion.5
  148.4 0.1 constant_dynamic-update-slice_fusion.4
  148.5 0.1 constant_dynamic-update-slice_fusion.3
  148.5 1.2 constant_dynamic-update-slice_fusion.2
  149.7 1.2 constant_dynamic-update-slice_fusion.1
  150.9 0.1 constant_dynamic-update-slice_fusion
  151.0 0.0 copy-start.1
  151.0 4.6 %copy-done.1 = bf16[1536,1,4096]{2,0,1:T(8,128)(2,1)} copy-done((bf16[1536,1,4096]{2,0,1:T(8,128)(2,1)}, bf16[1536,1,4096]{2,0,1:T(8,128)(2,1)S(1)}, u32[]{:S(2)}) %copy-start.1) | copy-done | bytes 12582936
  155.5 2.2 fusion.10
  157.8 0.0 copy-done
  157.8 13.4 %fusion.4 = bf16[768,1,4096]{2,0,1:T(8,128)(2,1)} fusion(bf16[1,192,4096]{2,1,0:T(8,128)(2,1)S(1)} %copy-done, f32[768,1,192]{0,2,1:T(8,128)S(1)} %fusion.10, bf16[1,192,4096]{2,1,0:T(8,128)(2,1)} %param.16, bf16[1536,1,4096]{2,0,1:T(8,128)(2,1)} %copy-done.1, s32[]{:T(128)S(6)} %select_n.59), kind=kOutput, calls=%fused_computation.6 | convolution fusion | flops 2419949568 | bytes 16318468 | tf_op jit(solution)/shard_map/ref,efd->red/dot_general | solution.py:77
  171.1 10.2 %reshape.122 = bf16[128,6,4096]{2,1,0:T(8,128)(2,1)} reshape(bf16[768,1,4096]{2,0,1:T(8,128)(2,1)} %fusion.4) | data formatting | bytes 12582912 | tf_op jit(solution)/shard_map/reshape | solution.py:78
  181.3 10.1 %all-to-all-start.1 = ((bf16[128,6,4096]{2,1,0:T(8,128)(2,1)}), bf16[128,6,4096]{2,1,0:T(8,128)(2,1)}, u32[]{:S(2)}, u32[]{:S(2)}) async-start(bf16[128,6,4096]{2,1,0:T(8,128)(2,1)} %reshape.122), calls=%async_computation.2 | async-start | bytes 16777216 | tf_op jit(solution)/shard_map/all_to_all | solution.py:81
  191.4 0.1 reduce_sum.56
  191.5 0.1 mul.76
  191.6 0.1 convert_reduce_fusion
  191.7 0.1 bitcast_divide_fusion
  191.8 0.0 copy-start.4
  191.8 174.4 %all-to-all-done.1 = bf16[128,6,4096]{2,1,0:T(8,128)(2,1)} async-done(((bf16[128,6,4096]{2,1,0:T(8,128)(2,1)}), bf16[128,6,4096]{2,1,0:T(8,128)(2,1)}, u32[]{:S(2)}, u32[]{:S(2)}) %all-to-all-start.1) | async-done | bytes 6291488 | tf_op jit(solution)/shard_map/all_to_all | solution.py:81
  366.2 10.2 %reshape.123 = bf16[8,96,4096]{2,1,0:T(8,128)(2,1)} reshape(bf16[128,6,4096]{2,1,0:T(8,128)(2,1)} %all-to-all-done.1) | data formatting | bytes 12582912 | tf_op jit(solution)/shard_map/reshape | solution.py:84
  376.4 4.0 %reduce_sum.59 = bf16[96,4096]{1,0:T(8,128)(2,1)S(1)} reduce(bf16[8,96,4096]{2,1,0:T(8,128)(2,1)} %reshape.123, bf16[]{:T(256)} %constant.93.clone.1), dimensions={0}, to_apply=%region_6.7 | reduce | flops 2752512 | bytes 7077890 | tf_op jit(solution)/shard_map/reduce_sum | solution.py:85
  380.4 0.9 gather_fusion
  381.3 0.4 multiply_reduce_fusion
  381.7 0.7 fusion.21
  (18 shorter events, 0.1 us)
Async XLA Ops:
  6.5 151.2 %copy-start = (bf16[1,192,4096]{2,1,0:T(8,128)(2,1)S(1)}, bf16[1,192,4096]{2,1,0:T(8,128)(2,1)}, u32[]{:S(2)}) copy-start(bf16[1,192,4096]{2,1,0:T(8,128)(2,1)} %param.17) | copy-start | bytes 4718596
  6.5 44.3 %reduce-scatter.2.cloned.1.call-start = ((), (), s32[]{:S(2)}) async-start(), calls=%async_computation.3 | async-start | bytes 589824 | tf_op jit(solution)/shard_map/reduce_scatter | solution.py:50
  72.5 17.8 %collective-permute-start = (bf16[96,1,4096]{2,0,1:T(8,128)(2,1)S(1)}, bf16[96,1,4096]{2,0,1:T(8,128)(2,1)S(1)}, u32[]{:S(2)}, u32[]{:S(2)}) collective-permute-start(bf16[96,1,4096]{2,0,1:T(8,128)(2,1)S(1)} %reshape.116), channel_id=1, source_target_pairs={{0,16},{16,32},{32,48},{48,64},{64,80},{80,96},{96,112},{112,0},{1... | collective-permute-start | bytes 2359304 | tf_op jit(solution)/shard_map/ppermute | solution.py:69
  90.2 17.7 %collective-permute-start.1 = (bf16[96,1,4096]{2,0,1:T(8,128)(2,1)S(1)}, bf16[96,1,4096]{2,0,1:T(8,128)(2,1)S(1)}, u32[]{:S(2)}, u32[]{:S(2)}) collective-permute-start(bf16[96,1,4096]{2,0,1:T(8,128)(2,1)S(1)} %collective-permute-done), channel_id=1, source_target_pairs={{0,16},{16,32},{32,48},{48,64},{64,80},{80,96},{96,112},{112,0},{1... | collective-permute-start | bytes 2359304 | tf_op jit(solution)/shard_map/ppermute | solution.py:69
  90.2 17.7 %collective-permute-start.4 = (bf16[96,1,4096]{2,0,1:T(8,128)(2,1)S(1)}, bf16[96,1,4096]{2,0,1:T(8,128)(2,1)}, u32[]{:S(2)}, u32[]{:S(2)}) collective-permute-start(bf16[96,1,4096]{2,0,1:T(8,128)(2,1)S(1)} %reshape.116), channel_id=1, source_target_pairs={{0,112},{16,0},{32,16},{48,32},{64,48},{80,64},{96,80},{112,96},{1... | collective-permute-start | bytes 2359304 | tf_op jit(solution)/shard_map/ppermute | solution.py:71
  107.9 0.9 copy-start.2
  108.0 18.3 %collective-permute-start.2 = (bf16[96,1,4096]{2,0,1:T(8,128)(2,1)S(1)}, bf16[96,1,4096]{2,0,1:T(8,128)(2,1)}, u32[]{:S(2)}, u32[]{:S(2)}) collective-permute-start(bf16[96,1,4096]{2,0,1:T(8,128)(2,1)S(1)} %collective-permute-done.1), channel_id=1, source_target_pairs={{0,16},{16,32},{32,48},{48,64},{64,80},{80,96},{96,112},{112,0},{1... | collective-permute-start | bytes 2359304 | tf_op jit(solution)/shard_map/ppermute | solution.py:69
  108.8 18.2 %collective-permute-start.5 = (bf16[96,1,4096]{2,0,1:T(8,128)(2,1)}, bf16[96,1,4096]{2,0,1:T(8,128)(2,1)}, u32[]{:S(2)}, u32[]{:S(2)}) collective-permute-start(bf16[96,1,4096]{2,0,1:T(8,128)(2,1)} %collective-permute-done.4), channel_id=1, source_target_pairs={{0,112},{16,0},{32,16},{48,32},{64,48},{80,64},{96,80},{112,96},{1... | collective-permute-start | bytes 2359304 | tf_op jit(solution)/shard_map/ppermute | solution.py:71
  126.3 13.5 %collective-permute-start.3 = (bf16[96,1,4096]{2,0,1:T(8,128)(2,1)}, bf16[96,1,4096]{2,0,1:T(8,128)(2,1)}, u32[]{:S(2)}, u32[]{:S(2)}) collective-permute-start(bf16[96,1,4096]{2,0,1:T(8,128)(2,1)} %collective-permute-done.2), channel_id=1, source_target_pairs={{0,16},{16,32},{32,48},{48,64},{64,80},{80,96},{96,112},{112,0},{1... | collective-permute-start | bytes 2359304 | tf_op jit(solution)/shard_map/ppermute | solution.py:69
  126.3 22.0 %copy-start.3 = (bf16[96,1,4096]{2,0,1:T(8,128)(2,1)S(1)}, bf16[96,1,4096]{2,0,1:T(8,128)(2,1)}, u32[]{:S(2)}) copy-start(bf16[96,1,4096]{2,0,1:T(8,128)(2,1)} %copy-done.2) | copy-start | bytes 2359300
  126.3 29.3 %copy-start.8 = (bf16[1,192,4096]{2,1,0:T(8,128)(2,1)S(1)}, bf16[1,192,4096]{2,1,0:T(8,128)(2,1)}, u32[]{:S(2)}) copy-start(bf16[1,192,4096]{2,1,0:T(8,128)(2,1)} %param.15) | copy-start | bytes 4718596
  127.0 18.9 %collective-permute-start.6 = (bf16[96,1,4096]{2,0,1:T(8,128)(2,1)}, bf16[96,1,4096]{2,0,1:T(8,128)(2,1)S(1)}, u32[]{:S(2)}, u32[]{:S(2)}) collective-permute-start(bf16[96,1,4096]{2,0,1:T(8,128)(2,1)} %collective-permute-done.5), channel_id=1, source_target_pairs={{0,112},{16,0},{32,16},{48,32},{64,48},{80,64},{96,80},{112,96},{1... | collective-permute-start | bytes 2359304 | tf_op jit(solution)/shard_map/ppermute | solution.py:71
  151.0 4.6 %copy-start.1 = (bf16[1536,1,4096]{2,0,1:T(8,128)(2,1)}, bf16[1536,1,4096]{2,0,1:T(8,128)(2,1)S(1)}, u32[]{:S(2)}) copy-start(bf16[1536,1,4096]{2,0,1:T(8,128)(2,1)S(1)} %constant_dynamic-update-slice_fusion) | copy-start | bytes 37748740
  171.1 20.4 %copy-start.7 = (s32[1,8,8]{2,1,0:T(8,128)S(1)}, s32[1,8,8]{2,1,0:T(8,128)}, u32[]{:S(2)}) copy-start(s32[1,8,8]{2,1,0:T(8,128)} %param.14) | copy-start | bytes 772
  171.1 20.6 %copy-start.6 = (s32[1,8,8]{2,1,0:T(8,128)S(1)}, s32[1,8,8]{2,1,0:T(8,128)}, u32[]{:S(2)}) copy-start(s32[1,8,8]{2,1,0:T(8,128)} %param.13) | copy-start | bytes 772
  181.3 184.9 %all-to-all-start.1 = ((bf16[128,6,4096]{2,1,0:T(8,128)(2,1)}), bf16[128,6,4096]{2,1,0:T(8,128)(2,1)}, u32[]{:S(2)}, u32[]{:S(2)}) async-start(bf16[128,6,4096]{2,1,0:T(8,128)(2,1)} %reshape.122), calls=%async_computation.2 | async-start | bytes 16777216 | tf_op jit(solution)/shard_map/all_to_all | solution.py:81
  191.8 189.9 %copy-start.4 = (bf16[1,8,4096]{2,1,0:T(8,128)(2,1)S(1)}, bf16[1,8,4096]{2,1,0:T(8,128)(2,1)}, u32[]{:S(2)}) copy-start(bf16[1,8,4096]{2,1,0:T(8,128)(2,1)} %param.11) | copy-start | bytes 196612
  191.8 189.9 %copy-start.5 = (bf16[8,4096]{1,0:T(8,128)(2,1)S(1)}, bf16[8,4096]{1,0:T(8,128)(2,1)}, u32[]{:S(2)}) copy-start(bf16[8,4096]{1,0:T(8,128)(2,1)} %reduce-scatter.2.cloned.1.call-done) | copy-start | bytes 196612
Sparse Core Ops, SparseCore 0:
  10.7 40.1 reduce-scatter.1
